TPU v7x, 512 devices: a whole 4x4x16 slice. The times are simulated.
512 devices in a mesh: dp: 8 (over y, core), ctx: 64 (over z, x).
Axes of the slice: x: 4, y: 4, z: 16, core: 2. Of those that a mesh axis runs over, the one named last changes fastest.
Arguments:
- query_in: bfloat16 [8, 8192, 1792], P('dp', 'ctx'), may hold values from -8 to 8
- key_in: bfloat16 [8, 8192, 256], P('dp', 'ctx'), may hold values from -4 to 4
- value_input: bfloat16 [8, 8192, 256], P('dp', 'ctx'), may hold values from -4 to 4
- output_gradient: bfloat16 [8, 8192, 1792], P('dp', 'ctx'), may hold values from -5 to 5
- doc_ids: int32 [8, 8192], P('dp', 'ctx'), may hold values from 0 to 1, as said below
- query_bias: float32 [1792], replicated, may hold values from -2 to 2
Outputs:
- attended: bfloat16 [8, 8192, 1792], P('dp', 'ctx')
- grad_query: bfloat16 [8, 8192, 1792], P('dp', 'ctx')
- key_gradient: bfloat16 [8, 8192, 256], P('dp', 'ctx')
- value_gradient: bfloat16 [8, 8192, 256], P('dp', 'ctx')
- grad_bias: float32 [1792], replicated
Inputs may be any that keep to these rules, and one draw needn't show every extreme that they name: `doc_ids`: ids never fall along a sequence; each of the 2 documents of a sequence holds 2048 to 6144 tokens, and together they fill all 8192 tokens.
All inputs are finite; a program needn't handle non-finite values.
Results may differ from a plain program's by a relative error of at most 0.019.
Values may be sent and summed in bfloat16 or wider, within the bound.
A program may use at most 64 MiB of HBM per device.

v0:
```python
import math
import jax
import jax.numpy as jnp
from jax import lax
from jax.sharding import PartitionSpec as P

QUERY_HEADS = 14
KEY_VALUE_HEADS = 2
HEAD_SIZE = 128
GROUP_SIZE = 7
BLK = 128
WB = 16


def passed_along(value, axis, steps):
    count = lax.axis_size(axis)
    first, last = (max(0, -steps), min(count, count - steps))
    return lax.ppermute(value, axis, [(source, source + steps) for source in range(first, last)])


def split_pack(packed_block):
    head_size_width = KEY_VALUE_HEADS * HEAD_SIZE
    key_head_rows = packed_block[:, :head_size_width].reshape(
        packed_block.shape[0], KEY_VALUE_HEADS, HEAD_SIZE
    )
    value_head_rows = packed_block[:, head_size_width:].reshape(
        packed_block.shape[0], KEY_VALUE_HEADS, HEAD_SIZE
    )
    return (key_head_rows, value_head_rows)


def local(query_in, key_in, value_input, output_gradient, doc_ids, query_bias):
    sharded_rows = query_in.shape[1]
    ctx_count = lax.axis_size("ctx")
    ctx_rank = lax.axis_index("ctx")
    score_scale = 1.0 / math.sqrt(HEAD_SIZE)
    blocks_here = sharded_rows // BLK
    window_slots = min((WB - 1 + blocks_here - 1) // blocks_here, ctx_count - 1) + 1
    group_slots = max(1, min(window_slots, 512 // sharded_rows))
    group_count = -(-window_slots // group_slots)
    padded_slots = group_count * group_slots
    grouped_rows = group_slots * sharded_rows
    packed_width = 2 * KEY_VALUE_HEADS * HEAD_SIZE
    query_rows = (query_in[0].astype(jnp.float32) + query_bias).astype(jnp.bfloat16)
    query_head_rows = query_rows.reshape(sharded_rows, KEY_VALUE_HEADS, GROUP_SIZE, HEAD_SIZE)
    gradient_heads = output_gradient[0].reshape(
        sharded_rows, KEY_VALUE_HEADS, GROUP_SIZE, HEAD_SIZE
    )
    own_pack = jnp.concatenate([key_in[0], value_input[0]], axis=1)
    own_docs = doc_ids[0]
    query_pos = ctx_rank * sharded_rows + jnp.arange(sharded_rows, dtype=jnp.int32)
    first_pack = jnp.concatenate(
        [own_pack[None], jnp.zeros((window_slots - 1, sharded_rows, packed_width), jnp.bfloat16)],
        axis=0,
    )
    first_docs = jnp.concatenate(
        [own_docs[None], jnp.zeros((window_slots - 1, sharded_rows), jnp.int32)], axis=0
    )

    def pass_on(step_index, running):
        stored_pack, stored_docs, moving_pack, moving_docs = running
        moving_pack, moving_docs = passed_along((moving_pack, moving_docs), "ctx", 1)
        stored_pack = lax.dynamic_update_index_in_dim(stored_pack, moving_pack, step_index, 0)
        stored_docs = lax.dynamic_update_index_in_dim(stored_docs, moving_docs, step_index, 0)
        return (stored_pack, stored_docs, moving_pack, moving_docs)

    window_pack, window_docs, _, _ = lax.fori_loop(
        1, window_slots, pass_on, (first_pack, first_docs, own_pack, own_docs)
    )
    spare_slots = padded_slots - window_slots
    window_pack = jnp.concatenate(
        [window_pack, jnp.zeros((spare_slots, sharded_rows, packed_width), jnp.bfloat16)], axis=0
    )
    window_pack = window_pack.reshape(group_count, grouped_rows, packed_width)
    window_docs = jnp.concatenate(
        [window_docs, jnp.zeros((spare_slots, sharded_rows), jnp.int32)], axis=0
    )
    window_docs = window_docs.reshape(group_count, grouped_rows)
    group_ids = jnp.arange(group_count, dtype=jnp.int32)

    def group_mask(group_index, docs_block):
        key_index = jnp.arange(grouped_rows, dtype=jnp.int32)
        slot_index = group_index * group_slots + key_index // sharded_rows
        key_pos = (ctx_rank - slot_index) * sharded_rows + key_index % sharded_rows
        inside = ((slot_index < window_slots) & (key_pos >= 0))[None, :]
        causal = key_pos[None, :] <= query_pos[:, None]
        near = query_pos[:, None] // BLK - key_pos[None, :] // BLK < WB
        same_doc = own_docs[:, None] == docs_block[None, :]
        return inside & causal & near & same_doc

    def group_scores(packed_block, allowed):
        key_head_rows, value_head_rows = split_pack(packed_block)
        scores = (
            jnp.einsum(
                "qgnd,kgd->gnqk", query_head_rows, key_head_rows, preferred_element_type=jnp.float32
            )
            * score_scale
        )
        return (jnp.where(allowed[None, None], scores, -jnp.inf), key_head_rows, value_head_rows)

    def forward_work(running, packed_block, allowed):
        row_max, row_sum, weighted = running
        scores, key_head_rows, value_head_rows = group_scores(packed_block, allowed)
        new_max = jnp.maximum(row_max, jnp.max(scores, axis=-1))
        rescale = jnp.exp(row_max - new_max)
        weights = jnp.exp(scores - new_max[..., None])
        row_sum = row_sum * rescale + jnp.sum(weights, axis=-1)
        weighted = weighted * rescale[..., None] + jnp.einsum(
            "gnqk,kgd->gnqd", weights, value_head_rows.astype(jnp.float32)
        )
        return (new_max, row_sum, weighted)

    def forward_step(running, inputs):
        packed_block, docs_block, group_index = inputs
        allowed = group_mask(group_index, docs_block)
        running = forward_work(running, packed_block, allowed)
        return (running, None)

    statistics_shape = (KEY_VALUE_HEADS, GROUP_SIZE, sharded_rows)
    start_stats = (
        jnp.full(statistics_shape, -jnp.inf, jnp.float32),
        jnp.zeros(statistics_shape, jnp.float32),
        jnp.zeros(statistics_shape + (HEAD_SIZE,), jnp.float32),
    )
    (row_max, row_sum, weighted), _ = lax.scan(
        forward_step, start_stats, (window_pack, window_docs, group_ids)
    )
    log_total = row_max + jnp.log(row_sum)
    attended = jnp.transpose(weighted / row_sum[..., None], (2, 0, 1, 3)).astype(jnp.bfloat16)
    row_dot = jnp.einsum(
        "qgnd,qgnd->gnq", gradient_heads, attended, preferred_element_type=jnp.float32
    )

    def backward_work(grad_query, packed_block, allowed):
        scores, key_head_rows, value_head_rows = group_scores(packed_block, allowed)
        attend = jnp.exp(scores - log_total[..., None])
        grad_prob = jnp.einsum(
            "qgnd,kgd->gnqk", gradient_heads, value_head_rows, preferred_element_type=jnp.float32
        )
        grad_score = (attend * (grad_prob - row_dot[..., None])).astype(jnp.bfloat16)
        grad_query = grad_query + jnp.einsum(
            "gnqk,kgd->qgnd", grad_score, key_head_rows, preferred_element_type=jnp.float32
        )
        key_gradient = (
            jnp.einsum(
                "gnqk,qgnd->kgd", grad_score, query_head_rows, preferred_element_type=jnp.float32
            )
            * score_scale
        )
        value_gradient = jnp.einsum(
            "gnqk,qgnd->kgd",
            attend.astype(jnp.bfloat16),
            gradient_heads,
            preferred_element_type=jnp.float32,
        )
        partial_value = jnp.concatenate(
            [
                key_gradient.reshape(grouped_rows, KEY_VALUE_HEADS * HEAD_SIZE),
                value_gradient.reshape(grouped_rows, KEY_VALUE_HEADS * HEAD_SIZE),
            ],
            axis=1,
        )
        return (grad_query, partial_value)

    def backward_step(grad_query, inputs):
        packed_block, docs_block, group_index = inputs
        allowed = group_mask(group_index, docs_block)
        return backward_work(grad_query, packed_block, allowed)

    grad_query, partials = lax.scan(
        backward_step,
        jnp.zeros((sharded_rows, KEY_VALUE_HEADS, GROUP_SIZE, HEAD_SIZE), jnp.float32),
        (window_pack, window_docs, group_ids),
    )
    partials = partials.reshape(padded_slots, sharded_rows, packed_width)
    query_grad = (grad_query * score_scale).reshape(sharded_rows, QUERY_HEADS * HEAD_SIZE)

    def return_partial(step_index, running):
        returned = passed_along(running, "ctx", -1)
        return returned + lax.dynamic_index_in_dim(
            partials, window_slots - 1 - step_index, 0, keepdims=False
        )

    summed_total = lax.fori_loop(1, window_slots, return_partial, partials[window_slots - 1])
    key_gradient = summed_total[:, : KEY_VALUE_HEADS * HEAD_SIZE].astype(jnp.bfloat16)
    value_gradient = summed_total[:, KEY_VALUE_HEADS * HEAD_SIZE :].astype(jnp.bfloat16)
    grad_bias = lax.psum(jnp.sum(query_grad, axis=0), ("dp", "ctx"))
    attended_out = attended.reshape(sharded_rows, QUERY_HEADS * HEAD_SIZE)
    return (
        attended_out[None],
        query_grad.astype(jnp.bfloat16)[None],
        key_gradient[None],
        value_gradient[None],
        grad_bias,
    )


def solution(mesh):
    placed = (
        P("dp", "ctx", None),
        P("dp", "ctx", None),
        P("dp", "ctx", None),
        P("dp", "ctx", None),
        P("dp", "ctx"),
        P(),
    )
    return jax.shard_map(
        local,
        mesh=mesh,
        in_specs=placed,
        out_specs=(
            P("dp", "ctx", None),
            P("dp", "ctx", None),
            P("dp", "ctx", None),
            P("dp", "ctx", None),
            P(),
        ),
        check_vma=False,
    )
```

profile of v0, /device:TPU:1, one launch (start us, length us, event | category | flops | bytes accessed | tf_op | source)
XLA Modules:
  0.0 563.7 jit_solution(16847469983181574787)
XLA Ops:
  8.9 138.4 %while.72 = (s32[]{:T(128)}, bf16[16,128,512]{2,1,0:T(8,128)(2,1)}, s32[16,128]{1,0:T(8,128)S(1)}, bf16[128,512]{1,0:T(8,128)(2,1)S(1)}, s32[128]{0:T(128)S(1)}, /*index=5*/s32[]{:T(128)}, s32[]{:T(128)}, s32[]{:T(128)}) while((s32[]{:T(128)}, bf16[16,128,512]{2,1,0:T(8,128)(2,1)}, s32[16,128]{1,0:T(8,128)S(1)}, ...), condition=%wide.region_1.2_spmd, body=%wide.region_0.1_spmd.sunk | while | flops 5 | bytes 1052879 | solution.py:67
  8.9 4.1 collective-permute-start
  17.5 3.6 collective-permute-start
  29.2 4.8 collective-permute-start.1
  35.5 3.9 collective-permute-start
  39.4 3.7 collective-permute-start.1
  44.5 3.9 collective-permute-start
  48.4 3.7 collective-permute-start.1
  53.5 3.6 collective-permute-start
  57.1 4.0 collective-permute-start.1
  62.6 3.6 collective-permute-start
  66.1 4.0 collective-permute-start.1
  71.6 3.6 collective-permute-start
  75.2 4.0 collective-permute-start.1
  80.6 3.6 collective-permute-start
  84.2 4.0 collective-permute-start.1
  89.7 3.6 collective-permute-start
  93.2 4.3 collective-permute-start.1
  99.0 3.6 collective-permute-start
  102.5 4.8 collective-permute-start.1
  108.8 3.6 collective-permute-start
  112.4 4.3 collective-permute-start.1
  118.1 3.9 collective-permute-start
  122.0 3.7 collective-permute-start.1
  127.1 3.9 collective-permute-start
  131.0 4.5 collective-permute-start.1
  137.0 3.6 collective-permute-start
  140.5 5.3 collective-permute-start.1
  147.3 4.1 copy.51
  151.5 23.1 %while.74 = (s32[]{:T(128)}, f32[2,7,128]{2,1,0:T(8,128)S(1)}, f32[2,7,128]{2,1,0:T(8,128)S(1)}, f32[2,7,128,128]{3,2,1,0:T(8,128)S(1)}, s32[4]{0:T(128)S(1)}, /...) while((s32[]{:T(128)}, f32[2,7,128]{2,1,0:T(8,128)S(1)}, ...), condition=%wide.region_5.6_spmd.clone.clone.clone, body=%wide.region_2.5_spmd.clone.clone.clone.sunk | while | flops 480120704 | bytes 16320205 | solution.py:125
  179.3 42.8 %while.75 = (s32[]{:T(128)}, f32[128,2,7,128]{0,3,2,1:T(8,128)S(1)}, f32[4,512,512]{2,1,0:T(8,128)}, bf16[4,512,512]{1,2,0:T(8,128)(2,1)}, s32[4]{0:T(128)S(1)},...) while((s32[]{:T(128)}, ...), condition=%wide.region_7.8_spmd.clone.clone.clone, body=%wide.region_6.7_spmd.clone.clone.clone.sunk | while | flops 1184918656 | bytes 30644960 | solution.py:170
  223.1 163.2 %while.73 = (s32[]{:T(128)}, f32[128,512]{1,0:T(8,128)S(1)}, f32[16,128,512]{2,1,0:T(8,128)}, s32[]{:T(128)}, s32[]{:T(128)}, /*index=5*/s32[]{:T(128)}, s32[]{:T(128)}) while((s32[]{:T(128)}, f32[128,512]{1,0:T(8,128)S(1)}, f32[16,128,512]{2,1,0:T(8,128)}, s32[]{:T(128)}, s32[]{:T(128)}, /*index=5*/s32[]{:T(128)}, s32[]{:T(128)}) %tuple.177), condition=%wide.region_9.10_spmd, body=%wide.region_8.9_spmd.sunk | while | flops 65542 | bytes 1835175 | solution.py:184
  224.4 6.0 %collective-permute-done.2 = f32[128,512]{1,0:T(8,128)S(1)} collective-permute-done((f32[128,512]{1,0:T(8,128)S(1)}, f32[128,512]{1,0:T(8,128)S(1)}, u32[]{:S(2)}, u32[]{:S(2)}) %collective-permute-start.2) | collective-permute-done | bytes 262176 | tf_op jit(solution)/shard_map/while/body/eval_jaxpr/ppermute | solution.py:18
  232.7 7.8 %collective-permute-done.2 = f32[128,512]{1,0:T(8,128)S(1)} collective-permute-done((f32[128,512]{1,0:T(8,128)S(1)}, f32[128,512]{1,0:T(8,128)S(1)}, u32[]{:S(2)}, u32[]{:S(2)}) %collective-permute-start.2) | collective-permute-done | bytes 262176 | tf_op jit(solution)/shard_map/while/body/eval_jaxpr/ppermute | solution.py:18
  242.8 7.7 %collective-permute-done.2 = f32[128,512]{1,0:T(8,128)S(1)} collective-permute-done((f32[128,512]{1,0:T(8,128)S(1)}, f32[128,512]{1,0:T(8,128)S(1)}, u32[]{:S(2)}, u32[]{:S(2)}) %collective-permute-start.2) | collective-permute-done | bytes 262176 | tf_op jit(solution)/shard_map/while/body/eval_jaxpr/ppermute | solution.py:18
  252.8 10.2 %collective-permute-done.2 = f32[128,512]{1,0:T(8,128)S(1)} collective-permute-done((f32[128,512]{1,0:T(8,128)S(1)}, f32[128,512]{1,0:T(8,128)S(1)}, u32[]{:S(2)}, u32[]{:S(2)}) %collective-permute-start.2) | collective-permute-done | bytes 262176 | tf_op jit(solution)/shard_map/while/body/eval_jaxpr/ppermute | solution.py:18
  265.3 11.4 %collective-permute-done.2 = f32[128,512]{1,0:T(8,128)S(1)} collective-permute-done((f32[128,512]{1,0:T(8,128)S(1)}, f32[128,512]{1,0:T(8,128)S(1)}, u32[]{:S(2)}, u32[]{:S(2)}) %collective-permute-start.2) | collective-permute-done | bytes 262176 | tf_op jit(solution)/shard_map/while/body/eval_jaxpr/ppermute | solution.py:18
  279.0 9.2 %collective-permute-done.2 = f32[128,512]{1,0:T(8,128)S(1)} collective-permute-done((f32[128,512]{1,0:T(8,128)S(1)}, f32[128,512]{1,0:T(8,128)S(1)}, u32[]{:S(2)}, u32[]{:S(2)}) %collective-permute-start.2) | collective-permute-done | bytes 262176 | tf_op jit(solution)/shard_map/while/body/eval_jaxpr/ppermute | solution.py:18
  290.5 7.4 %collective-permute-done.2 = f32[128,512]{1,0:T(8,128)S(1)} collective-permute-done((f32[128,512]{1,0:T(8,128)S(1)}, f32[128,512]{1,0:T(8,128)S(1)}, u32[]{:S(2)}, u32[]{:S(2)}) %collective-permute-start.2) | collective-permute-done | bytes 262176 | tf_op jit(solution)/shard_map/while/body/eval_jaxpr/ppermute | solution.py:18
  300.1 6.8 %collective-permute-done.2 = f32[128,512]{1,0:T(8,128)S(1)} collective-permute-done((f32[128,512]{1,0:T(8,128)S(1)}, f32[128,512]{1,0:T(8,128)S(1)}, u32[]{:S(2)}, u32[]{:S(2)}) %collective-permute-start.2) | collective-permute-done | bytes 262176 | tf_op jit(solution)/shard_map/while/body/eval_jaxpr/ppermute | solution.py:18
  309.3 7.6 %collective-permute-done.2 = f32[128,512]{1,0:T(8,128)S(1)} collective-permute-done((f32[128,512]{1,0:T(8,128)S(1)}, f32[128,512]{1,0:T(8,128)S(1)}, u32[]{:S(2)}, u32[]{:S(2)}) %collective-permute-start.2) | collective-permute-done | bytes 262176 | tf_op jit(solution)/shard_map/while/body/eval_jaxpr/ppermute | solution.py:18
  319.2 7.9 %collective-permute-done.2 = f32[128,512]{1,0:T(8,128)S(1)} collective-permute-done((f32[128,512]{1,0:T(8,128)S(1)}, f32[128,512]{1,0:T(8,128)S(1)}, u32[]{:S(2)}, u32[]{:S(2)}) %collective-permute-start.2) | collective-permute-done | bytes 262176 | tf_op jit(solution)/shard_map/while/body/eval_jaxpr/ppermute | solution.py:18
  329.4 7.9 %collective-permute-done.2 = f32[128,512]{1,0:T(8,128)S(1)} collective-permute-done((f32[128,512]{1,0:T(8,128)S(1)}, f32[128,512]{1,0:T(8,128)S(1)}, u32[]{:S(2)}, u32[]{:S(2)}) %collective-permute-start.2) | collective-permute-done | bytes 262176 | tf_op jit(solution)/shard_map/while/body/eval_jaxpr/ppermute | solution.py:18
  339.7 7.9 %collective-permute-done.2 = f32[128,512]{1,0:T(8,128)S(1)} collective-permute-done((f32[128,512]{1,0:T(8,128)S(1)}, f32[128,512]{1,0:T(8,128)S(1)}, u32[]{:S(2)}, u32[]{:S(2)}) %collective-permute-start.2) | collective-permute-done | bytes 262176 | tf_op jit(solution)/shard_map/while/body/eval_jaxpr/ppermute | solution.py:18
  349.9 8.8 %collective-permute-done.2 = f32[128,512]{1,0:T(8,128)S(1)} collective-permute-done((f32[128,512]{1,0:T(8,128)S(1)}, f32[128,512]{1,0:T(8,128)S(1)}, u32[]{:S(2)}, u32[]{:S(2)}) %collective-permute-start.2) | collective-permute-done | bytes 262176 | tf_op jit(solution)/shard_map/while/body/eval_jaxpr/ppermute | solution.py:18
  361.0 10.4 %collective-permute-done.2 = f32[128,512]{1,0:T(8,128)S(1)} collective-permute-done((f32[128,512]{1,0:T(8,128)S(1)}, f32[128,512]{1,0:T(8,128)S(1)}, u32[]{:S(2)}, u32[]{:S(2)}) %collective-permute-start.2) | collective-permute-done | bytes 262176 | tf_op jit(solution)/shard_map/while/body/eval_jaxpr/ppermute | solution.py:18
  373.7 11.5 %collective-permute-done.2 = f32[128,512]{1,0:T(8,128)S(1)} collective-permute-done((f32[128,512]{1,0:T(8,128)S(1)}, f32[128,512]{1,0:T(8,128)S(1)}, u32[]{:S(2)}, u32[]{:S(2)}) %collective-permute-start.2) | collective-permute-done | bytes 262176 | tf_op jit(solution)/shard_map/while/body/eval_jaxpr/ppermute | solution.py:18
  387.3 175.4 %psum.7 = f32[1792]{0:T(1024)} all-reduce(f32[1792]{0:T(1024)S(1)} %reduce_sum.25), channel_id=1, replica_groups=mesh['dp'=8,'ctx'=64] {'dp','ctx'}, use_global_device_ids=true, to_apply=%region_11.12 | all-reduce | flops 1792 | bytes 14336 | tf_op jit(solution)/shard_map/psum | solution.py:187
  (274 shorter events, 140.9 us)
Async XLA Ops:
  8.9 142.6 %copy-start.1 = (s32[1,128]{1,0:T(1,128)S(1)}, s32[1,128]{1,0:T(1,128)}, u32[]{:S(2)}) copy-start(s32[1,128]{1,0:T(1,128)} %param.18) | copy-start | bytes 1540
  8.9 7.9 %collective-permute-start = (bf16[128,512]{1,0:T(8,128)(2,1)S(1)}, bf16[128,512]{1,0:T(8,128)(2,1)S(1)}, u32[]{:S(2)}, u32[]{:S(2)}) collective-permute-start(bf16[128,512]{1,0:T(8,128)(2,1)S(1)} %get-tuple-element.1222), channel_id=1, source_target_pairs={{0,1},{1,2},{2,3},{3,4},{4,5},{5,6},{6,7},{7,8},{8,9},{9,10},{10,1... | collective-permute-start | bytes 393224 | tf_op jit(solution)/shard_map/while/body/eval_jaxpr/ppermute | solution.py:18
  13.0 3.8 collective-permute-start.1
  17.5 7.4 %collective-permute-start = (bf16[128,512]{1,0:T(8,128)(2,1)S(1)}, bf16[128,512]{1,0:T(8,128)(2,1)S(1)}, u32[]{:S(2)}, u32[]{:S(2)}) collective-permute-start(bf16[128,512]{1,0:T(8,128)(2,1)S(1)} %get-tuple-element.1222), channel_id=1, source_target_pairs={{0,1},{1,2},{2,3},{3,4},{4,5},{5,6},{6,7},{7,8},{8,9},{9,10},{10,1... | collective-permute-start | bytes 393224 | tf_op jit(solution)/shard_map/while/body/eval_jaxpr/ppermute | solution.py:18
  21.1 3.8 collective-permute-start.1
  25.7 9.1 %collective-permute-start = (bf16[128,512]{1,0:T(8,128)(2,1)S(1)}, bf16[128,512]{1,0:T(8,128)(2,1)S(1)}, u32[]{:S(2)}, u32[]{:S(2)}) collective-permute-start(bf16[128,512]{1,0:T(8,128)(2,1)S(1)} %get-tuple-element.1222), channel_id=1, source_target_pairs={{0,1},{1,2},{2,3},{3,4},{4,5},{5,6},{6,7},{7,8},{8,9},{9,10},{10,1... | collective-permute-start | bytes 393224 | tf_op jit(solution)/shard_map/while/body/eval_jaxpr/ppermute | solution.py:18
  29.2 5.5 collective-permute-start.1
  35.5 8.3 %collective-permute-start = (bf16[128,512]{1,0:T(8,128)(2,1)S(1)}, bf16[128,512]{1,0:T(8,128)(2,1)S(1)}, u32[]{:S(2)}, u32[]{:S(2)}) collective-permute-start(bf16[128,512]{1,0:T(8,128)(2,1)S(1)} %get-tuple-element.1222), channel_id=1, source_target_pairs={{0,1},{1,2},{2,3},{3,4},{4,5},{5,6},{6,7},{7,8},{8,9},{9,10},{10,1... | collective-permute-start | bytes 393224 | tf_op jit(solution)/shard_map/while/body/eval_jaxpr/ppermute | solution.py:18
  39.4 4.4 collective-permute-start.1
  44.5 8.3 %collective-permute-start = (bf16[128,512]{1,0:T(8,128)(2,1)S(1)}, bf16[128,512]{1,0:T(8,128)(2,1)S(1)}, u32[]{:S(2)}, u32[]{:S(2)}) collective-permute-start(bf16[128,512]{1,0:T(8,128)(2,1)S(1)} %get-tuple-element.1222), channel_id=1, source_target_pairs={{0,1},{1,2},{2,3},{3,4},{4,5},{5,6},{6,7},{7,8},{8,9},{9,10},{10,1... | collective-permute-start | bytes 393224 | tf_op jit(solution)/shard_map/while/body/eval_jaxpr/ppermute | solution.py:18
  48.4 4.4 collective-permute-start.1
  53.5 8.3 %collective-permute-start = (bf16[128,512]{1,0:T(8,128)(2,1)S(1)}, bf16[128,512]{1,0:T(8,128)(2,1)S(1)}, u32[]{:S(2)}, u32[]{:S(2)}) collective-permute-start(bf16[128,512]{1,0:T(8,128)(2,1)S(1)} %get-tuple-element.1222), channel_id=1, source_target_pairs={{0,1},{1,2},{2,3},{3,4},{4,5},{5,6},{6,7},{7,8},{8,9},{9,10},{10,1... | collective-permute-start | bytes 393224 | tf_op jit(solution)/shard_map/while/body/eval_jaxpr/ppermute | solution.py:18
  57.1 4.7 collective-permute-start.1
  62.6 8.3 %collective-permute-start = (bf16[128,512]{1,0:T(8,128)(2,1)S(1)}, bf16[128,512]{1,0:T(8,128)(2,1)S(1)}, u32[]{:S(2)}, u32[]{:S(2)}) collective-permute-start(bf16[128,512]{1,0:T(8,128)(2,1)S(1)} %get-tuple-element.1222), channel_id=1, source_target_pairs={{0,1},{1,2},{2,3},{3,4},{4,5},{5,6},{6,7},{7,8},{8,9},{9,10},{10,1... | collective-permute-start | bytes 393224 | tf_op jit(solution)/shard_map/while/body/eval_jaxpr/ppermute | solution.py:18
  66.1 4.7 collective-permute-start.1
  71.6 8.3 %collective-permute-start = (bf16[128,512]{1,0:T(8,128)(2,1)S(1)}, bf16[128,512]{1,0:T(8,128)(2,1)S(1)}, u32[]{:S(2)}, u32[]{:S(2)}) collective-permute-start(bf16[128,512]{1,0:T(8,128)(2,1)S(1)} %get-tuple-element.1222), channel_id=1, source_target_pairs={{0,1},{1,2},{2,3},{3,4},{4,5},{5,6},{6,7},{7,8},{8,9},{9,10},{10,1... | collective-permute-start | bytes 393224 | tf_op jit(solution)/shard_map/while/body/eval_jaxpr/ppermute | solution.py:18
  75.2 4.7 collective-permute-start.1
  80.6 8.4 %collective-permute-start = (bf16[128,512]{1,0:T(8,128)(2,1)S(1)}, bf16[128,512]{1,0:T(8,128)(2,1)S(1)}, u32[]{:S(2)}, u32[]{:S(2)}) collective-permute-start(bf16[128,512]{1,0:T(8,128)(2,1)S(1)} %get-tuple-element.1222), channel_id=1, source_target_pairs={{0,1},{1,2},{2,3},{3,4},{4,5},{5,6},{6,7},{7,8},{8,9},{9,10},{10,1... | collective-permute-start | bytes 393224 | tf_op jit(solution)/shard_map/while/body/eval_jaxpr/ppermute | solution.py:18
  84.2 4.7 collective-permute-start.1
  89.7 8.6 %collective-permute-start = (bf16[128,512]{1,0:T(8,128)(2,1)S(1)}, bf16[128,512]{1,0:T(8,128)(2,1)S(1)}, u32[]{:S(2)}, u32[]{:S(2)}) collective-permute-start(bf16[128,512]{1,0:T(8,128)(2,1)S(1)} %get-tuple-element.1222), channel_id=1, source_target_pairs={{0,1},{1,2},{2,3},{3,4},{4,5},{5,6},{6,7},{7,8},{8,9},{9,10},{10,1... | collective-permute-start | bytes 393224 | tf_op jit(solution)/shard_map/while/body/eval_jaxpr/ppermute | solution.py:18
  93.2 5.0 collective-permute-start.1
  99.0 9.1 %collective-permute-start = (bf16[128,512]{1,0:T(8,128)(2,1)S(1)}, bf16[128,512]{1,0:T(8,128)(2,1)S(1)}, u32[]{:S(2)}, u32[]{:S(2)}) collective-permute-start(bf16[128,512]{1,0:T(8,128)(2,1)S(1)} %get-tuple-element.1222), channel_id=1, source_target_pairs={{0,1},{1,2},{2,3},{3,4},{4,5},{5,6},{6,7},{7,8},{8,9},{9,10},{10,1... | collective-permute-start | bytes 393224 | tf_op jit(solution)/shard_map/while/body/eval_jaxpr/ppermute | solution.py:18
  102.5 5.5 collective-permute-start.1
  108.8 8.6 %collective-permute-start = (bf16[128,512]{1,0:T(8,128)(2,1)S(1)}, bf16[128,512]{1,0:T(8,128)(2,1)S(1)}, u32[]{:S(2)}, u32[]{:S(2)}) collective-permute-start(bf16[128,512]{1,0:T(8,128)(2,1)S(1)} %get-tuple-element.1222), channel_id=1, source_target_pairs={{0,1},{1,2},{2,3},{3,4},{4,5},{5,6},{6,7},{7,8},{8,9},{9,10},{10,1... | collective-permute-start | bytes 393224 | tf_op jit(solution)/shard_map/while/body/eval_jaxpr/ppermute | solution.py:18
  112.4 5.0 collective-permute-start.1
  118.1 8.3 %collective-permute-start = (bf16[128,512]{1,0:T(8,128)(2,1)S(1)}, bf16[128,512]{1,0:T(8,128)(2,1)S(1)}, u32[]{:S(2)}, u32[]{:S(2)}) collective-permute-start(bf16[128,512]{1,0:T(8,128)(2,1)S(1)} %get-tuple-element.1222), channel_id=1, source_target_pairs={{0,1},{1,2},{2,3},{3,4},{4,5},{5,6},{6,7},{7,8},{8,9},{9,10},{10,1... | collective-permute-start | bytes 393224 | tf_op jit(solution)/shard_map/while/body/eval_jaxpr/ppermute | solution.py:18
  122.0 4.4 collective-permute-start.1
  127.1 9.1 %collective-permute-start = (bf16[128,512]{1,0:T(8,128)(2,1)S(1)}, bf16[128,512]{1,0:T(8,128)(2,1)S(1)}, u32[]{:S(2)}, u32[]{:S(2)}) collective-permute-start(bf16[128,512]{1,0:T(8,128)(2,1)S(1)} %get-tuple-element.1222), channel_id=1, source_target_pairs={{0,1},{1,2},{2,3},{3,4},{4,5},{5,6},{6,7},{7,8},{8,9},{9,10},{10,1... | collective-permute-start | bytes 393224 | tf_op jit(solution)/shard_map/while/body/eval_jaxpr/ppermute | solution.py:18
  131.0 5.2 collective-permute-start.1
  137.0 9.7 %collective-permute-start = (bf16[128,512]{1,0:T(8,128)(2,1)S(1)}, bf16[128,512]{1,0:T(8,128)(2,1)S(1)}, u32[]{:S(2)}, u32[]{:S(2)}) collective-permute-start(bf16[128,512]{1,0:T(8,128)(2,1)S(1)} %get-tuple-element.1222), channel_id=1, source_target_pairs={{0,1},{1,2},{2,3},{3,4},{4,5},{5,6},{6,7},{7,8},{8,9},{9,10},{10,1... | collective-permute-start | bytes 393224 | tf_op jit(solution)/shard_map/while/body/eval_jaxpr/ppermute | solution.py:18
  140.5 6.1 %collective-permute-start.1 = (s32[128]{0:T(128)S(1)}, s32[128]{0:T(128)S(1)}, u32[]{:S(2)}, u32[]{:S(2)}) collective-permute-start(s32[128]{0:T(128)S(1)} %get-tuple-element.1223), channel_id=1, source_target_pairs={{0,1},{1,2},{2,3},{3,4},{4,5},{5,6},{6,7},{7,8},{8,9},{9,10},{10,1... | collective-permute-start | bytes 1544 | tf_op jit(solution)/shard_map/while/body/eval_jaxpr/ppermute | solution.py:18
  174.6 1.0 copy-start
  223.1 7.3 %collective-permute-start.2 = (f32[128,512]{1,0:T(8,128)S(1)}, f32[128,512]{1,0:T(8,128)S(1)}, u32[]{:S(2)}, u32[]{:S(2)}) collective-permute-start(f32[128,512]{1,0:T(8,128)S(1)} %get-tuple-element.1333), channel_id=1, source_target_pairs={{1,0},{2,1},{3,2},{4,3},{5,4},{6,5},{7,6},{8,7},{9,8},{10,9},{11,1... | collective-permute-start | bytes 786440 | tf_op jit(solution)/shard_map/while/body/eval_jaxpr/ppermute | solution.py:18
  231.4 9.1 %collective-permute-start.2 = (f32[128,512]{1,0:T(8,128)S(1)}, f32[128,512]{1,0:T(8,128)S(1)}, u32[]{:S(2)}, u32[]{:S(2)}) collective-permute-start(f32[128,512]{1,0:T(8,128)S(1)} %get-tuple-element.1333), channel_id=1, source_target_pairs={{1,0},{2,1},{3,2},{4,3},{5,4},{6,5},{7,6},{8,7},{9,8},{10,9},{11,1... | collective-permute-start | bytes 786440 | tf_op jit(solution)/shard_map/while/body/eval_jaxpr/ppermute | solution.py:18
  241.5 9.0 %collective-permute-start.2 = (f32[128,512]{1,0:T(8,128)S(1)}, f32[128,512]{1,0:T(8,128)S(1)}, u32[]{:S(2)}, u32[]{:S(2)}) collective-permute-start(f32[128,512]{1,0:T(8,128)S(1)} %get-tuple-element.1333), channel_id=1, source_target_pairs={{1,0},{2,1},{3,2},{4,3},{5,4},{6,5},{7,6},{8,7},{9,8},{10,9},{11,1... | collective-permute-start | bytes 786440 | tf_op jit(solution)/shard_map/while/body/eval_jaxpr/ppermute | solution.py:18
  251.5 11.5 %collective-permute-start.2 = (f32[128,512]{1,0:T(8,128)S(1)}, f32[128,512]{1,0:T(8,128)S(1)}, u32[]{:S(2)}, u32[]{:S(2)}) collective-permute-start(f32[128,512]{1,0:T(8,128)S(1)} %get-tuple-element.1333), channel_id=1, source_target_pairs={{1,0},{2,1},{3,2},{4,3},{5,4},{6,5},{7,6},{8,7},{9,8},{10,9},{11,1... | collective-permute-start | bytes 786440 | tf_op jit(solution)/shard_map/while/body/eval_jaxpr/ppermute | solution.py:18
  264.0 12.7 %collective-permute-start.2 = (f32[128,512]{1,0:T(8,128)S(1)}, f32[128,512]{1,0:T(8,128)S(1)}, u32[]{:S(2)}, u32[]{:S(2)}) collective-permute-start(f32[128,512]{1,0:T(8,128)S(1)} %get-tuple-element.1333), channel_id=1, source_target_pairs={{1,0},{2,1},{3,2},{4,3},{5,4},{6,5},{7,6},{8,7},{9,8},{10,9},{11,1... | collective-permute-start | bytes 786440 | tf_op jit(solution)/shard_map/while/body/eval_jaxpr/ppermute | solution.py:18
  277.7 10.5 %collective-permute-start.2 = (f32[128,512]{1,0:T(8,128)S(1)}, f32[128,512]{1,0:T(8,128)S(1)}, u32[]{:S(2)}, u32[]{:S(2)}) collective-permute-start(f32[128,512]{1,0:T(8,128)S(1)} %get-tuple-element.1333), channel_id=1, source_target_pairs={{1,0},{2,1},{3,2},{4,3},{5,4},{6,5},{7,6},{8,7},{9,8},{10,9},{11,1... | collective-permute-start | bytes 786440 | tf_op jit(solution)/shard_map/while/body/eval_jaxpr/ppermute | solution.py:18
  289.2 8.7 %collective-permute-start.2 = (f32[128,512]{1,0:T(8,128)S(1)}, f32[128,512]{1,0:T(8,128)S(1)}, u32[]{:S(2)}, u32[]{:S(2)}) collective-permute-start(f32[128,512]{1,0:T(8,128)S(1)} %get-tuple-element.1333), channel_id=1, source_target_pairs={{1,0},{2,1},{3,2},{4,3},{5,4},{6,5},{7,6},{8,7},{9,8},{10,9},{11,1... | collective-permute-start | bytes 786440 | tf_op jit(solution)/shard_map/while/body/eval_jaxpr/ppermute | solution.py:18
  298.8 8.1 %collective-permute-start.2 = (f32[128,512]{1,0:T(8,128)S(1)}, f32[128,512]{1,0:T(8,128)S(1)}, u32[]{:S(2)}, u32[]{:S(2)}) collective-permute-start(f32[128,512]{1,0:T(8,128)S(1)} %get-tuple-element.1333), channel_id=1, source_target_pairs={{1,0},{2,1},{3,2},{4,3},{5,4},{6,5},{7,6},{8,7},{9,8},{10,9},{11,1... | collective-permute-start | bytes 786440 | tf_op jit(solution)/shard_map/while/body/eval_jaxpr/ppermute | solution.py:18
  308.0 8.9 %collective-permute-start.2 = (f32[128,512]{1,0:T(8,128)S(1)}, f32[128,512]{1,0:T(8,128)S(1)}, u32[]{:S(2)}, u32[]{:S(2)}) collective-permute-start(f32[128,512]{1,0:T(8,128)S(1)} %get-tuple-element.1333), channel_id=1, source_target_pairs={{1,0},{2,1},{3,2},{4,3},{5,4},{6,5},{7,6},{8,7},{9,8},{10,9},{11,1... | collective-permute-start | bytes 786440 | tf_op jit(solution)/shard_map/while/body/eval_jaxpr/ppermute | solution.py:18
  317.9 9.2 %collective-permute-start.2 = (f32[128,512]{1,0:T(8,128)S(1)}, f32[128,512]{1,0:T(8,128)S(1)}, u32[]{:S(2)}, u32[]{:S(2)}) collective-permute-start(f32[128,512]{1,0:T(8,128)S(1)} %get-tuple-element.1333), channel_id=1, source_target_pairs={{1,0},{2,1},{3,2},{4,3},{5,4},{6,5},{7,6},{8,7},{9,8},{10,9},{11,1... | collective-permute-start | bytes 786440 | tf_op jit(solution)/shard_map/while/body/eval_jaxpr/ppermute | solution.py:18
  328.1 9.2 %collective-permute-start.2 = (f32[128,512]{1,0:T(8,128)S(1)}, f32[128,512]{1,0:T(8,128)S(1)}, u32[]{:S(2)}, u32[]{:S(2)}) collective-permute-start(f32[128,512]{1,0:T(8,128)S(1)} %get-tuple-element.1333), channel_id=1, source_target_pairs={{1,0},{2,1},{3,2},{4,3},{5,4},{6,5},{7,6},{8,7},{9,8},{10,9},{11,1... | collective-permute-start | bytes 786440 | tf_op jit(solution)/shard_map/while/body/eval_jaxpr/ppermute | solution.py:18
  338.4 9.2 %collective-permute-start.2 = (f32[128,512]{1,0:T(8,128)S(1)}, f32[128,512]{1,0:T(8,128)S(1)}, u32[]{:S(2)}, u32[]{:S(2)}) collective-permute-start(f32[128,512]{1,0:T(8,128)S(1)} %get-tuple-element.1333), channel_id=1, source_target_pairs={{1,0},{2,1},{3,2},{4,3},{5,4},{6,5},{7,6},{8,7},{9,8},{10,9},{11,1... | collective-permute-start | bytes 786440 | tf_op jit(solution)/shard_map/while/body/eval_jaxpr/ppermute | solution.py:18
  348.6 10.1 %collective-permute-start.2 = (f32[128,512]{1,0:T(8,128)S(1)}, f32[128,512]{1,0:T(8,128)S(1)}, u32[]{:S(2)}, u32[]{:S(2)}) collective-permute-start(f32[128,512]{1,0:T(8,128)S(1)} %get-tuple-element.1333), channel_id=1, source_target_pairs={{1,0},{2,1},{3,2},{4,3},{5,4},{6,5},{7,6},{8,7},{9,8},{10,9},{11,1... | collective-permute-start | bytes 786440 | tf_op jit(solution)/shard_map/while/body/eval_jaxpr/ppermute | solution.py:18
  359.7 11.7 %collective-permute-start.2 = (f32[128,512]{1,0:T(8,128)S(1)}, f32[128,512]{1,0:T(8,128)S(1)}, u32[]{:S(2)}, u32[]{:S(2)}) collective-permute-start(f32[128,512]{1,0:T(8,128)S(1)} %get-tuple-element.1333), channel_id=1, source_target_pairs={{1,0},{2,1},{3,2},{4,3},{5,4},{6,5},{7,6},{8,7},{9,8},{10,9},{11,1... | collective-permute-start | bytes 786440 | tf_op jit(solution)/shard_map/while/body/eval_jaxpr/ppermute | solution.py:18
  372.4 12.8 %collective-permute-start.2 = (f32[128,512]{1,0:T(8,128)S(1)}, f32[128,512]{1,0:T(8,128)S(1)}, u32[]{:S(2)}, u32[]{:S(2)}) collective-permute-start(f32[128,512]{1,0:T(8,128)S(1)} %get-tuple-element.1333), channel_id=1, source_target_pairs={{1,0},{2,1},{3,2},{4,3},{5,4},{6,5},{7,6},{8,7},{9,8},{10,9},{11,1... | collective-permute-start | bytes 786440 | tf_op jit(solution)/shard_map/while/body/eval_jaxpr/ppermute | solution.py:18
where the time goes:
time: 567 us; the launch traced here: 564 us
  blocking collectives  175 us (31%)
  waiting for transfers between devices  139 us (25%)
  starting transfers between devices  136 us (24%)
  local copies, waits for them, and re-layouts  47.1 us (8%)
  matrix products  34.2 us (6%)
  other arithmetic  24 us (4%)
  loops' own time  6.87 us (1%)
    psum x1, blocking collectives, local(): grad_bias = lax.psum(jnp.sum(query_grad, axis=0), ('dp', 'ctx'))  175 us
    ppermute x45, waiting for transfers between devices, passed_along(): lax.ppermute(value, axis, [(source, source + steps) for source in range(f...  139 us
    ppermute x45, starting transfers between devices, passed_along(): lax.ppermute(value, axis, [(source, source + steps) for source in range(f...  136 us
    add x15, other arithmetic, return_partial(): returned + lax.dynamic_index_in_dim(partials, window_slots - 1 - step_ind...  14.8 us
  transfers between devices with their start and end apart: 45, of which 30 were waited for; matrix products, arithmetic and copies ran while one was open for 0% of the time, Pallas kernels for 0%

commit v1 on v0

--- a/solution.py
+++ b/solution.py
@@ -184,7 +184,7 @@
     summed_total = lax.fori_loop(1, window_slots, return_partial, partials[window_slots - 1])
     key_gradient = summed_total[:, : KEY_VALUE_HEADS * HEAD_SIZE].astype(jnp.bfloat16)
     value_gradient = summed_total[:, KEY_VALUE_HEADS * HEAD_SIZE :].astype(jnp.bfloat16)
-    grad_bias = lax.psum(jnp.sum(query_grad, axis=0), ("dp", "ctx"))
+    grad_bias = lax.psum(lax.psum(jnp.sum(query_grad, axis=0), "dp"), "ctx")
     attended_out = attended.reshape(sharded_rows, QUERY_HEADS * HEAD_SIZE)
     return (
         attended_out[None],

time: 567 us -> 615 us (1.085)
  the two profiles are of different devices: /device:TPU:1 before, /device:TPU:256 now
where the time goes in v1:
time: 615 us; the launch traced here: 612 us
  starting transfers between devices  170 us (28%)
  waiting for transfers between devices  170 us (28%)
  blocking collectives  159 us (26%)
  local copies, waits for them, and re-layouts  47 us (8%)
  matrix products  34.2 us (6%)
  other arithmetic  23.9 us (4%)
  loops' own time  6.9 us (1%)
    ppermute x45, waiting for transfers between devices, passed_along(): lax.ppermute(value, axis, [(source, source + steps) for source in range(f...  170 us
    ppermute x45, starting transfers between devices, passed_along(): lax.ppermute(value, axis, [(source, source + steps) for source in range(f...  170 us
    psum x2, blocking collectives, local(): grad_bias = lax.psum(lax.psum(jnp.sum(query_grad, axis=0), 'dp'), 'ctx')  159 us
    add x15, other arithmetic, return_partial(): returned + lax.dynamic_index_in_dim(partials, window_slots - 1 - step_ind...  14.8 us
  transfers between devices with their start and end apart: 45, of which 30 were waited for; matrix products, arithmetic and copies ran while one was open for 0% of the time, Pallas kernels for 0%

profile of v1, /device:TPU:256, one launch (start us, length us, event | category | flops | bytes accessed | tf_op | source)
XLA Modules:
  0.0 612.0 jit_solution(8247892324866899004)
XLA Ops:
  8.9 173.2 %while.72 = (s32[]{:T(128)}, bf16[16,128,512]{2,1,0:T(8,128)(2,1)}, s32[16,128]{1,0:T(8,128)S(1)}, bf16[128,512]{1,0:T(8,128)(2,1)S(1)}, s32[128]{0:T(128)S(1)}, /*index=5*/s32[]{:T(128)}, s32[]{:T(128)}, s32[]{:T(128)}) while((s32[]{:T(128)}, bf16[16,128,512]{2,1,0:T(8,128)(2,1)}, s32[16,128]{1,0:T(8,128)S(1)}, ...), condition=%wide.region_1.2_spmd, body=%wide.region_0.1_spmd.sunk | while | flops 5 | bytes 1052879 | solution.py:67
  15.8 5.3 collective-permute-done.1
  25.7 6.8 %collective-permute-done.1 = s32[128]{0:T(128)S(1)} collective-permute-done((s32[128]{0:T(128)S(1)}, s32[128]{0:T(128)S(1)}, u32[]{:S(2)}, u32[]{:S(2)}) %collective-permute-start.1) | collective-permute-done | bytes 544 | tf_op jit(solution)/shard_map/while/body/eval_jaxpr/ppermute | solution.py:18
  37.1 6.8 %collective-permute-done.1 = s32[128]{0:T(128)S(1)} collective-permute-done((s32[128]{0:T(128)S(1)}, s32[128]{0:T(128)S(1)}, u32[]{:S(2)}, u32[]{:S(2)}) %collective-permute-start.1) | collective-permute-done | bytes 544 | tf_op jit(solution)/shard_map/while/body/eval_jaxpr/ppermute | solution.py:18
  48.5 6.8 %collective-permute-done.1 = s32[128]{0:T(128)S(1)} collective-permute-done((s32[128]{0:T(128)S(1)}, s32[128]{0:T(128)S(1)}, u32[]{:S(2)}, u32[]{:S(2)}) %collective-permute-start.1) | collective-permute-done | bytes 544 | tf_op jit(solution)/shard_map/while/body/eval_jaxpr/ppermute | solution.py:18
  59.9 6.8 %collective-permute-done.1 = s32[128]{0:T(128)S(1)} collective-permute-done((s32[128]{0:T(128)S(1)}, s32[128]{0:T(128)S(1)}, u32[]{:S(2)}, u32[]{:S(2)}) %collective-permute-start.1) | collective-permute-done | bytes 544 | tf_op jit(solution)/shard_map/while/body/eval_jaxpr/ppermute | solution.py:18
  71.3 6.8 %collective-permute-done.1 = s32[128]{0:T(128)S(1)} collective-permute-done((s32[128]{0:T(128)S(1)}, s32[128]{0:T(128)S(1)}, u32[]{:S(2)}, u32[]{:S(2)}) %collective-permute-start.1) | collective-permute-done | bytes 544 | tf_op jit(solution)/shard_map/while/body/eval_jaxpr/ppermute | solution.py:18
  82.7 6.8 %collective-permute-done.1 = s32[128]{0:T(128)S(1)} collective-permute-done((s32[128]{0:T(128)S(1)}, s32[128]{0:T(128)S(1)}, u32[]{:S(2)}, u32[]{:S(2)}) %collective-permute-start.1) | collective-permute-done | bytes 544 | tf_op jit(solution)/shard_map/while/body/eval_jaxpr/ppermute | solution.py:18
  94.1 7.0 %collective-permute-done.1 = s32[128]{0:T(128)S(1)} collective-permute-done((s32[128]{0:T(128)S(1)}, s32[128]{0:T(128)S(1)}, u32[]{:S(2)}, u32[]{:S(2)}) %collective-permute-start.1) | collective-permute-done | bytes 544 | tf_op jit(solution)/shard_map/while/body/eval_jaxpr/ppermute | solution.py:18
  105.7 7.4 %collective-permute-done.1 = s32[128]{0:T(128)S(1)} collective-permute-done((s32[128]{0:T(128)S(1)}, s32[128]{0:T(128)S(1)}, u32[]{:S(2)}, u32[]{:S(2)}) %collective-permute-start.1) | collective-permute-done | bytes 544 | tf_op jit(solution)/shard_map/while/body/eval_jaxpr/ppermute | solution.py:18
  117.6 6.8 %collective-permute-done.1 = s32[128]{0:T(128)S(1)} collective-permute-done((s32[128]{0:T(128)S(1)}, s32[128]{0:T(128)S(1)}, u32[]{:S(2)}, u32[]{:S(2)}) %collective-permute-start.1) | collective-permute-done | bytes 544 | tf_op jit(solution)/shard_map/while/body/eval_jaxpr/ppermute | solution.py:18
  129.0 6.8 %collective-permute-done.1 = s32[128]{0:T(128)S(1)} collective-permute-done((s32[128]{0:T(128)S(1)}, s32[128]{0:T(128)S(1)}, u32[]{:S(2)}, u32[]{:S(2)}) %collective-permute-start.1) | collective-permute-done | bytes 544 | tf_op jit(solution)/shard_map/while/body/eval_jaxpr/ppermute | solution.py:18
  140.4 6.8 %collective-permute-done.1 = s32[128]{0:T(128)S(1)} collective-permute-done((s32[128]{0:T(128)S(1)}, s32[128]{0:T(128)S(1)}, u32[]{:S(2)}, u32[]{:S(2)}) %collective-permute-start.1) | collective-permute-done | bytes 544 | tf_op jit(solution)/shard_map/while/body/eval_jaxpr/ppermute | solution.py:18
  151.8 6.8 %collective-permute-done.1 = s32[128]{0:T(128)S(1)} collective-permute-done((s32[128]{0:T(128)S(1)}, s32[128]{0:T(128)S(1)}, u32[]{:S(2)}, u32[]{:S(2)}) %collective-permute-start.1) | collective-permute-done | bytes 544 | tf_op jit(solution)/shard_map/while/body/eval_jaxpr/ppermute | solution.py:18
  163.2 6.8 %collective-permute-done.1 = s32[128]{0:T(128)S(1)} collective-permute-done((s32[128]{0:T(128)S(1)}, s32[128]{0:T(128)S(1)}, u32[]{:S(2)}, u32[]{:S(2)}) %collective-permute-start.1) | collective-permute-done | bytes 544 | tf_op jit(solution)/shard_map/while/body/eval_jaxpr/ppermute | solution.py:18
  174.6 6.8 %collective-permute-done.1 = s32[128]{0:T(128)S(1)} collective-permute-done((s32[128]{0:T(128)S(1)}, s32[128]{0:T(128)S(1)}, u32[]{:S(2)}, u32[]{:S(2)}) %collective-permute-start.1) | collective-permute-done | bytes 544 | tf_op jit(solution)/shard_map/while/body/eval_jaxpr/ppermute | solution.py:18
  182.1 4.1 copy.51
  186.2 23.1 %while.74 = (s32[]{:T(128)}, f32[2,7,128]{2,1,0:T(8,128)S(1)}, f32[2,7,128]{2,1,0:T(8,128)S(1)}, f32[2,7,128,128]{3,2,1,0:T(8,128)S(1)}, s32[4]{0:T(128)S(1)}, /...) while((s32[]{:T(128)}, f32[2,7,128]{2,1,0:T(8,128)S(1)}, ...), condition=%wide.region_5.6_spmd.clone.clone.clone, body=%wide.region_2.5_spmd.clone.clone.clone.sunk | while | flops 480120704 | bytes 16320205 | solution.py:125
  214.0 42.8 %while.75 = (s32[]{:T(128)}, f32[128,2,7,128]{0,3,2,1:T(8,128)S(1)}, f32[4,512,512]{2,1,0:T(8,128)}, bf16[4,512,512]{1,2,0:T(8,128)(2,1)}, s32[4]{0:T(128)S(1)},...) while((s32[]{:T(128)}, ...), condition=%wide.region_7.8_spmd.clone.clone.clone, body=%wide.region_6.7_spmd.clone.clone.clone.sunk | while | flops 1184918656 | bytes 30644960 | solution.py:170
  257.8 193.2 %while.73 = (s32[]{:T(128)}, f32[128,512]{1,0:T(8,128)S(1)}, f32[16,128,512]{2,1,0:T(8,128)}, s32[]{:T(128)}, s32[]{:T(128)}, /*index=5*/s32[]{:T(128)}, s32[]{:T(128)}) while((s32[]{:T(128)}, f32[128,512]{1,0:T(8,128)S(1)}, f32[16,128,512]{2,1,0:T(8,128)}, s32[]{:T(128)}, s32[]{:T(128)}, /*index=5*/s32[]{:T(128)}, s32[]{:T(128)}) %tuple.177), condition=%wide.region_9.10_spmd, body=%wide.region_8.9_spmd.sunk | while | flops 65542 | bytes 1835175 | solution.py:184
  257.8 3.9 collective-permute-start.2
  261.7 6.1 collective-permute-done.2
  268.8 5.5 collective-permute-start.2
  274.3 4.0 collective-permute-done.2
  279.3 7.6 %collective-permute-start.2 = (f32[128,512]{1,0:T(8,128)S(1)}, f32[128,512]{1,0:T(8,128)S(1)}, u32[]{:S(2)}, u32[]{:S(2)}) collective-permute-start(f32[128,512]{1,0:T(8,128)S(1)} %get-tuple-element.1333), channel_id=1, source_target_pairs={{1,0},{2,1},{3,2},{4,3},{5,4},{6,5},{7,6},{8,7},{9,8},{10,9},{11,1... | collective-permute-start | bytes 786440 | tf_op jit(solution)/shard_map/while/body/eval_jaxpr/ppermute | solution.py:18
  286.9 4.4 collective-permute-done.2
  292.2 7.7 %collective-permute-start.2 = (f32[128,512]{1,0:T(8,128)S(1)}, f32[128,512]{1,0:T(8,128)S(1)}, u32[]{:S(2)}, u32[]{:S(2)}) collective-permute-start(f32[128,512]{1,0:T(8,128)S(1)} %get-tuple-element.1333), channel_id=1, source_target_pairs={{1,0},{2,1},{3,2},{4,3},{5,4},{6,5},{7,6},{8,7},{9,8},{10,9},{11,1... | collective-permute-start | bytes 786440 | tf_op jit(solution)/shard_map/while/body/eval_jaxpr/ppermute | solution.py:18
  300.0 5.5 collective-permute-done.2
  306.5 7.7 %collective-permute-start.2 = (f32[128,512]{1,0:T(8,128)S(1)}, f32[128,512]{1,0:T(8,128)S(1)}, u32[]{:S(2)}, u32[]{:S(2)}) collective-permute-start(f32[128,512]{1,0:T(8,128)S(1)} %get-tuple-element.1333), channel_id=1, source_target_pairs={{1,0},{2,1},{3,2},{4,3},{5,4},{6,5},{7,6},{8,7},{9,8},{10,9},{11,1... | collective-permute-start | bytes 786440 | tf_op jit(solution)/shard_map/while/body/eval_jaxpr/ppermute | solution.py:18
  314.2 6.6 %collective-permute-done.2 = f32[128,512]{1,0:T(8,128)S(1)} collective-permute-done((f32[128,512]{1,0:T(8,128)S(1)}, f32[128,512]{1,0:T(8,128)S(1)}, u32[]{:S(2)}, u32[]{:S(2)}) %collective-permute-start.2) | collective-permute-done | bytes 262176 | tf_op jit(solution)/shard_map/while/body/eval_jaxpr/ppermute | solution.py:18
  321.8 7.7 %collective-permute-start.2 = (f32[128,512]{1,0:T(8,128)S(1)}, f32[128,512]{1,0:T(8,128)S(1)}, u32[]{:S(2)}, u32[]{:S(2)}) collective-permute-start(f32[128,512]{1,0:T(8,128)S(1)} %get-tuple-element.1333), channel_id=1, source_target_pairs={{1,0},{2,1},{3,2},{4,3},{5,4},{6,5},{7,6},{8,7},{9,8},{10,9},{11,1... | collective-permute-start | bytes 786440 | tf_op jit(solution)/shard_map/while/body/eval_jaxpr/ppermute | solution.py:18
  329.5 5.8 collective-permute-done.2
  336.3 7.7 %collective-permute-start.2 = (f32[128,512]{1,0:T(8,128)S(1)}, f32[128,512]{1,0:T(8,128)S(1)}, u32[]{:S(2)}, u32[]{:S(2)}) collective-permute-start(f32[128,512]{1,0:T(8,128)S(1)} %get-tuple-element.1333), channel_id=1, source_target_pairs={{1,0},{2,1},{3,2},{4,3},{5,4},{6,5},{7,6},{8,7},{9,8},{10,9},{11,1... | collective-permute-start | bytes 786440 | tf_op jit(solution)/shard_map/while/body/eval_jaxpr/ppermute | solution.py:18
  344.1 5.0 collective-permute-done.2
  350.1 7.7 %collective-permute-start.2 = (f32[128,512]{1,0:T(8,128)S(1)}, f32[128,512]{1,0:T(8,128)S(1)}, u32[]{:S(2)}, u32[]{:S(2)}) collective-permute-start(f32[128,512]{1,0:T(8,128)S(1)} %get-tuple-element.1333), channel_id=1, source_target_pairs={{1,0},{2,1},{3,2},{4,3},{5,4},{6,5},{7,6},{8,7},{9,8},{10,9},{11,1... | collective-permute-start | bytes 786440 | tf_op jit(solution)/shard_map/while/body/eval_jaxpr/ppermute | solution.py:18
  357.8 4.1 collective-permute-done.2
  362.8 7.7 %collective-permute-start.2 = (f32[128,512]{1,0:T(8,128)S(1)}, f32[128,512]{1,0:T(8,128)S(1)}, u32[]{:S(2)}, u32[]{:S(2)}) collective-permute-start(f32[128,512]{1,0:T(8,128)S(1)} %get-tuple-element.1333), channel_id=1, source_target_pairs={{1,0},{2,1},{3,2},{4,3},{5,4},{6,5},{7,6},{8,7},{9,8},{10,9},{11,1... | collective-permute-start | bytes 786440 | tf_op jit(solution)/shard_map/while/body/eval_jaxpr/ppermute | solution.py:18
  370.6 3.9 collective-permute-done.2
  375.4 7.7 %collective-permute-start.2 = (f32[128,512]{1,0:T(8,128)S(1)}, f32[128,512]{1,0:T(8,128)S(1)}, u32[]{:S(2)}, u32[]{:S(2)}) collective-permute-start(f32[128,512]{1,0:T(8,128)S(1)} %get-tuple-element.1333), channel_id=1, source_target_pairs={{1,0},{2,1},{3,2},{4,3},{5,4},{6,5},{7,6},{8,7},{9,8},{10,9},{11,1... | collective-permute-start | bytes 786440 | tf_op jit(solution)/shard_map/while/body/eval_jaxpr/ppermute | solution.py:18
  383.1 3.9 collective-permute-done.2
  388.0 7.7 %collective-permute-start.2 = (f32[128,512]{1,0:T(8,128)S(1)}, f32[128,512]{1,0:T(8,128)S(1)}, u32[]{:S(2)}, u32[]{:S(2)}) collective-permute-start(f32[128,512]{1,0:T(8,128)S(1)} %get-tuple-element.1333), channel_id=1, source_target_pairs={{1,0},{2,1},{3,2},{4,3},{5,4},{6,5},{7,6},{8,7},{9,8},{10,9},{11,1... | collective-permute-start | bytes 786440 | tf_op jit(solution)/shard_map/while/body/eval_jaxpr/ppermute | solution.py:18
  395.7 3.9 collective-permute-done.2
  400.6 7.7 %collective-permute-start.2 = (f32[128,512]{1,0:T(8,128)S(1)}, f32[128,512]{1,0:T(8,128)S(1)}, u32[]{:S(2)}, u32[]{:S(2)}) collective-permute-start(f32[128,512]{1,0:T(8,128)S(1)} %get-tuple-element.1333), channel_id=1, source_target_pairs={{1,0},{2,1},{3,2},{4,3},{5,4},{6,5},{7,6},{8,7},{9,8},{10,9},{11,1... | collective-permute-start | bytes 786440 | tf_op jit(solution)/shard_map/while/body/eval_jaxpr/ppermute | solution.py:18
  413.2 7.7 %collective-permute-start.2 = (f32[128,512]{1,0:T(8,128)S(1)}, f32[128,512]{1,0:T(8,128)S(1)}, u32[]{:S(2)}, u32[]{:S(2)}) collective-permute-start(f32[128,512]{1,0:T(8,128)S(1)} %get-tuple-element.1333), channel_id=1, source_target_pairs={{1,0},{2,1},{3,2},{4,3},{5,4},{6,5},{7,6},{8,7},{9,8},{10,9},{11,1... | collective-permute-start | bytes 786440 | tf_op jit(solution)/shard_map/while/body/eval_jaxpr/ppermute | solution.py:18
  425.8 7.7 %collective-permute-start.2 = (f32[128,512]{1,0:T(8,128)S(1)}, f32[128,512]{1,0:T(8,128)S(1)}, u32[]{:S(2)}, u32[]{:S(2)}) collective-permute-start(f32[128,512]{1,0:T(8,128)S(1)} %get-tuple-element.1333), channel_id=1, source_target_pairs={{1,0},{2,1},{3,2},{4,3},{5,4},{6,5},{7,6},{8,7},{9,8},{10,9},{11,1... | collective-permute-start | bytes 786440 | tf_op jit(solution)/shard_map/while/body/eval_jaxpr/ppermute | solution.py:18
  438.4 7.7 %collective-permute-start.2 = (f32[128,512]{1,0:T(8,128)S(1)}, f32[128,512]{1,0:T(8,128)S(1)}, u32[]{:S(2)}, u32[]{:S(2)}) collective-permute-start(f32[128,512]{1,0:T(8,128)S(1)} %get-tuple-element.1333), channel_id=1, source_target_pairs={{1,0},{2,1},{3,2},{4,3},{5,4},{6,5},{7,6},{8,7},{9,8},{10,9},{11,1... | collective-permute-start | bytes 786440 | tf_op jit(solution)/shard_map/while/body/eval_jaxpr/ppermute | solution.py:18
  452.0 12.7 %psum.14 = f32[1792]{0:T(1024)S(1)} all-reduce(f32[1792]{0:T(1024)S(1)} %reduce_sum.25), channel_id=1, replica_groups=mesh['dp'=8,'ctx'=64] {'dp'}, use_global_device_ids=true, to_apply=%region_11.12 | all-reduce | flops 1792 | bytes 14336 | tf_op jit(solution)/shard_map/psum | solution.py:187
  464.6 146.4 %psum.15 = f32[1792]{0:T(1024)} all-reduce(f32[1792]{0:T(1024)S(1)} %psum.14), channel_id=1, replica_groups=mesh['dp'=8,'ctx'=64] {'ctx'}, use_global_device_ids=true, to_apply=%region_12.13 | all-reduce | flops 1792 | bytes 14336 | tf_op jit(solution)/shard_map/psum | solution.py:187
  (275 shorter events, 177.0 us)
Async XLA Ops:
  8.9 177.3 %copy-start.1 = (s32[1,128]{1,0:T(1,128)S(1)}, s32[1,128]{1,0:T(1,128)}, u32[]{:S(2)}) copy-start(s32[1,128]{1,0:T(1,128)} %param.18) | copy-start | bytes 1540
  8.9 12.3 %collective-permute-start = (bf16[128,512]{1,0:T(8,128)(2,1)S(1)}, bf16[128,512]{1,0:T(8,128)(2,1)S(1)}, u32[]{:S(2)}, u32[]{:S(2)}) collective-permute-start(bf16[128,512]{1,0:T(8,128)(2,1)S(1)} %get-tuple-element.1222), channel_id=1, source_target_pairs={{0,1},{1,2},{2,3},{3,4},{4,5},{5,6},{6,7},{7,8},{8,9},{9,10},{10,1... | collective-permute-start | bytes 393224 | tf_op jit(solution)/shard_map/while/body/eval_jaxpr/ppermute | solution.py:18
  12.4 8.8 %collective-permute-start.1 = (s32[128]{0:T(128)S(1)}, s32[128]{0:T(128)S(1)}, u32[]{:S(2)}, u32[]{:S(2)}) collective-permute-start(s32[128]{0:T(128)S(1)} %get-tuple-element.1223), channel_id=1, source_target_pairs={{0,1},{1,2},{2,3},{3,4},{4,5},{5,6},{6,7},{7,8},{8,9},{9,10},{10,1... | collective-permute-start | bytes 1544 | tf_op jit(solution)/shard_map/while/body/eval_jaxpr/ppermute | solution.py:18
  21.9 10.7 %collective-permute-start = (bf16[128,512]{1,0:T(8,128)(2,1)S(1)}, bf16[128,512]{1,0:T(8,128)(2,1)S(1)}, u32[]{:S(2)}, u32[]{:S(2)}) collective-permute-start(bf16[128,512]{1,0:T(8,128)(2,1)S(1)} %get-tuple-element.1222), channel_id=1, source_target_pairs={{0,1},{1,2},{2,3},{3,4},{4,5},{5,6},{6,7},{7,8},{8,9},{9,10},{10,1... | collective-permute-start | bytes 393224 | tf_op jit(solution)/shard_map/while/body/eval_jaxpr/ppermute | solution.py:18
  23.8 8.8 %collective-permute-start.1 = (s32[128]{0:T(128)S(1)}, s32[128]{0:T(128)S(1)}, u32[]{:S(2)}, u32[]{:S(2)}) collective-permute-start(s32[128]{0:T(128)S(1)} %get-tuple-element.1223), channel_id=1, source_target_pairs={{0,1},{1,2},{2,3},{3,4},{4,5},{5,6},{6,7},{7,8},{8,9},{9,10},{10,1... | collective-permute-start | bytes 1544 | tf_op jit(solution)/shard_map/while/body/eval_jaxpr/ppermute | solution.py:18
  33.3 10.7 %collective-permute-start = (bf16[128,512]{1,0:T(8,128)(2,1)S(1)}, bf16[128,512]{1,0:T(8,128)(2,1)S(1)}, u32[]{:S(2)}, u32[]{:S(2)}) collective-permute-start(bf16[128,512]{1,0:T(8,128)(2,1)S(1)} %get-tuple-element.1222), channel_id=1, source_target_pairs={{0,1},{1,2},{2,3},{3,4},{4,5},{5,6},{6,7},{7,8},{8,9},{9,10},{10,1... | collective-permute-start | bytes 393224 | tf_op jit(solution)/shard_map/while/body/eval_jaxpr/ppermute | solution.py:18
  35.2 8.8 %collective-permute-start.1 = (s32[128]{0:T(128)S(1)}, s32[128]{0:T(128)S(1)}, u32[]{:S(2)}, u32[]{:S(2)}) collective-permute-start(s32[128]{0:T(128)S(1)} %get-tuple-element.1223), channel_id=1, source_target_pairs={{0,1},{1,2},{2,3},{3,4},{4,5},{5,6},{6,7},{7,8},{8,9},{9,10},{10,1... | collective-permute-start | bytes 1544 | tf_op jit(solution)/shard_map/while/body/eval_jaxpr/ppermute | solution.py:18
  44.7 10.7 %collective-permute-start = (bf16[128,512]{1,0:T(8,128)(2,1)S(1)}, bf16[128,512]{1,0:T(8,128)(2,1)S(1)}, u32[]{:S(2)}, u32[]{:S(2)}) collective-permute-start(bf16[128,512]{1,0:T(8,128)(2,1)S(1)} %get-tuple-element.1222), channel_id=1, source_target_pairs={{0,1},{1,2},{2,3},{3,4},{4,5},{5,6},{6,7},{7,8},{8,9},{9,10},{10,1... | collective-permute-start | bytes 393224 | tf_op jit(solution)/shard_map/while/body/eval_jaxpr/ppermute | solution.py:18
  46.6 8.8 %collective-permute-start.1 = (s32[128]{0:T(128)S(1)}, s32[128]{0:T(128)S(1)}, u32[]{:S(2)}, u32[]{:S(2)}) collective-permute-start(s32[128]{0:T(128)S(1)} %get-tuple-element.1223), channel_id=1, source_target_pairs={{0,1},{1,2},{2,3},{3,4},{4,5},{5,6},{6,7},{7,8},{8,9},{9,10},{10,1... | collective-permute-start | bytes 1544 | tf_op jit(solution)/shard_map/while/body/eval_jaxpr/ppermute | solution.py:18
  56.0 10.7 %collective-permute-start = (bf16[128,512]{1,0:T(8,128)(2,1)S(1)}, bf16[128,512]{1,0:T(8,128)(2,1)S(1)}, u32[]{:S(2)}, u32[]{:S(2)}) collective-permute-start(bf16[128,512]{1,0:T(8,128)(2,1)S(1)} %get-tuple-element.1222), channel_id=1, source_target_pairs={{0,1},{1,2},{2,3},{3,4},{4,5},{5,6},{6,7},{7,8},{8,9},{9,10},{10,1... | collective-permute-start | bytes 393224 | tf_op jit(solution)/shard_map/while/body/eval_jaxpr/ppermute | solution.py:18
  58.0 8.8 %collective-permute-start.1 = (s32[128]{0:T(128)S(1)}, s32[128]{0:T(128)S(1)}, u32[]{:S(2)}, u32[]{:S(2)}) collective-permute-start(s32[128]{0:T(128)S(1)} %get-tuple-element.1223), channel_id=1, source_target_pairs={{0,1},{1,2},{2,3},{3,4},{4,5},{5,6},{6,7},{7,8},{8,9},{9,10},{10,1... | collective-permute-start | bytes 1544 | tf_op jit(solution)/shard_map/while/body/eval_jaxpr/ppermute | solution.py:18
  67.4 10.7 %collective-permute-start = (bf16[128,512]{1,0:T(8,128)(2,1)S(1)}, bf16[128,512]{1,0:T(8,128)(2,1)S(1)}, u32[]{:S(2)}, u32[]{:S(2)}) collective-permute-start(bf16[128,512]{1,0:T(8,128)(2,1)S(1)} %get-tuple-element.1222), channel_id=1, source_target_pairs={{0,1},{1,2},{2,3},{3,4},{4,5},{5,6},{6,7},{7,8},{8,9},{9,10},{10,1... | collective-permute-start | bytes 393224 | tf_op jit(solution)/shard_map/while/body/eval_jaxpr/ppermute | solution.py:18
  69.3 8.8 %collective-permute-start.1 = (s32[128]{0:T(128)S(1)}, s32[128]{0:T(128)S(1)}, u32[]{:S(2)}, u32[]{:S(2)}) collective-permute-start(s32[128]{0:T(128)S(1)} %get-tuple-element.1223), channel_id=1, source_target_pairs={{0,1},{1,2},{2,3},{3,4},{4,5},{5,6},{6,7},{7,8},{8,9},{9,10},{10,1... | collective-permute-start | bytes 1544 | tf_op jit(solution)/shard_map/while/body/eval_jaxpr/ppermute | solution.py:18
  78.8 10.7 %collective-permute-start = (bf16[128,512]{1,0:T(8,128)(2,1)S(1)}, bf16[128,512]{1,0:T(8,128)(2,1)S(1)}, u32[]{:S(2)}, u32[]{:S(2)}) collective-permute-start(bf16[128,512]{1,0:T(8,128)(2,1)S(1)} %get-tuple-element.1222), channel_id=1, source_target_pairs={{0,1},{1,2},{2,3},{3,4},{4,5},{5,6},{6,7},{7,8},{8,9},{9,10},{10,1... | collective-permute-start | bytes 393224 | tf_op jit(solution)/shard_map/while/body/eval_jaxpr/ppermute | solution.py:18
  80.7 8.8 %collective-permute-start.1 = (s32[128]{0:T(128)S(1)}, s32[128]{0:T(128)S(1)}, u32[]{:S(2)}, u32[]{:S(2)}) collective-permute-start(s32[128]{0:T(128)S(1)} %get-tuple-element.1223), channel_id=1, source_target_pairs={{0,1},{1,2},{2,3},{3,4},{4,5},{5,6},{6,7},{7,8},{8,9},{9,10},{10,1... | collective-permute-start | bytes 1544 | tf_op jit(solution)/shard_map/while/body/eval_jaxpr/ppermute | solution.py:18
  90.2 10.9 %collective-permute-start = (bf16[128,512]{1,0:T(8,128)(2,1)S(1)}, bf16[128,512]{1,0:T(8,128)(2,1)S(1)}, u32[]{:S(2)}, u32[]{:S(2)}) collective-permute-start(bf16[128,512]{1,0:T(8,128)(2,1)S(1)} %get-tuple-element.1222), channel_id=1, source_target_pairs={{0,1},{1,2},{2,3},{3,4},{4,5},{5,6},{6,7},{7,8},{8,9},{9,10},{10,1... | collective-permute-start | bytes 393224 | tf_op jit(solution)/shard_map/while/body/eval_jaxpr/ppermute | solution.py:18
  92.1 9.0 %collective-permute-start.1 = (s32[128]{0:T(128)S(1)}, s32[128]{0:T(128)S(1)}, u32[]{:S(2)}, u32[]{:S(2)}) collective-permute-start(s32[128]{0:T(128)S(1)} %get-tuple-element.1223), channel_id=1, source_target_pairs={{0,1},{1,2},{2,3},{3,4},{4,5},{5,6},{6,7},{7,8},{8,9},{9,10},{10,1... | collective-permute-start | bytes 1544 | tf_op jit(solution)/shard_map/while/body/eval_jaxpr/ppermute | solution.py:18
  101.8 11.3 %collective-permute-start = (bf16[128,512]{1,0:T(8,128)(2,1)S(1)}, bf16[128,512]{1,0:T(8,128)(2,1)S(1)}, u32[]{:S(2)}, u32[]{:S(2)}) collective-permute-start(bf16[128,512]{1,0:T(8,128)(2,1)S(1)} %get-tuple-element.1222), channel_id=1, source_target_pairs={{0,1},{1,2},{2,3},{3,4},{4,5},{5,6},{6,7},{7,8},{8,9},{9,10},{10,1... | collective-permute-start | bytes 393224 | tf_op jit(solution)/shard_map/while/body/eval_jaxpr/ppermute | solution.py:18
  103.7 9.3 %collective-permute-start.1 = (s32[128]{0:T(128)S(1)}, s32[128]{0:T(128)S(1)}, u32[]{:S(2)}, u32[]{:S(2)}) collective-permute-start(s32[128]{0:T(128)S(1)} %get-tuple-element.1223), channel_id=1, source_target_pairs={{0,1},{1,2},{2,3},{3,4},{4,5},{5,6},{6,7},{7,8},{8,9},{9,10},{10,1... | collective-permute-start | bytes 1544 | tf_op jit(solution)/shard_map/while/body/eval_jaxpr/ppermute | solution.py:18
  113.7 10.7 %collective-permute-start = (bf16[128,512]{1,0:T(8,128)(2,1)S(1)}, bf16[128,512]{1,0:T(8,128)(2,1)S(1)}, u32[]{:S(2)}, u32[]{:S(2)}) collective-permute-start(bf16[128,512]{1,0:T(8,128)(2,1)S(1)} %get-tuple-element.1222), channel_id=1, source_target_pairs={{0,1},{1,2},{2,3},{3,4},{4,5},{5,6},{6,7},{7,8},{8,9},{9,10},{10,1... | collective-permute-start | bytes 393224 | tf_op jit(solution)/shard_map/while/body/eval_jaxpr/ppermute | solution.py:18
  115.7 8.8 %collective-permute-start.1 = (s32[128]{0:T(128)S(1)}, s32[128]{0:T(128)S(1)}, u32[]{:S(2)}, u32[]{:S(2)}) collective-permute-start(s32[128]{0:T(128)S(1)} %get-tuple-element.1223), channel_id=1, source_target_pairs={{0,1},{1,2},{2,3},{3,4},{4,5},{5,6},{6,7},{7,8},{8,9},{9,10},{10,1... | collective-permute-start | bytes 1544 | tf_op jit(solution)/shard_map/while/body/eval_jaxpr/ppermute | solution.py:18
  125.1 10.7 %collective-permute-start = (bf16[128,512]{1,0:T(8,128)(2,1)S(1)}, bf16[128,512]{1,0:T(8,128)(2,1)S(1)}, u32[]{:S(2)}, u32[]{:S(2)}) collective-permute-start(bf16[128,512]{1,0:T(8,128)(2,1)S(1)} %get-tuple-element.1222), channel_id=1, source_target_pairs={{0,1},{1,2},{2,3},{3,4},{4,5},{5,6},{6,7},{7,8},{8,9},{9,10},{10,1... | collective-permute-start | bytes 393224 | tf_op jit(solution)/shard_map/while/body/eval_jaxpr/ppermute | solution.py:18
  127.1 8.8 %collective-permute-start.1 = (s32[128]{0:T(128)S(1)}, s32[128]{0:T(128)S(1)}, u32[]{:S(2)}, u32[]{:S(2)}) collective-permute-start(s32[128]{0:T(128)S(1)} %get-tuple-element.1223), channel_id=1, source_target_pairs={{0,1},{1,2},{2,3},{3,4},{4,5},{5,6},{6,7},{7,8},{8,9},{9,10},{10,1... | collective-permute-start | bytes 1544 | tf_op jit(solution)/shard_map/while/body/eval_jaxpr/ppermute | solution.py:18
  136.5 10.7 %collective-permute-start = (bf16[128,512]{1,0:T(8,128)(2,1)S(1)}, bf16[128,512]{1,0:T(8,128)(2,1)S(1)}, u32[]{:S(2)}, u32[]{:S(2)}) collective-permute-start(bf16[128,512]{1,0:T(8,128)(2,1)S(1)} %get-tuple-element.1222), channel_id=1, source_target_pairs={{0,1},{1,2},{2,3},{3,4},{4,5},{5,6},{6,7},{7,8},{8,9},{9,10},{10,1... | collective-permute-start | bytes 393224 | tf_op jit(solution)/shard_map/while/body/eval_jaxpr/ppermute | solution.py:18
  138.4 8.8 %collective-permute-start.1 = (s32[128]{0:T(128)S(1)}, s32[128]{0:T(128)S(1)}, u32[]{:S(2)}, u32[]{:S(2)}) collective-permute-start(s32[128]{0:T(128)S(1)} %get-tuple-element.1223), channel_id=1, source_target_pairs={{0,1},{1,2},{2,3},{3,4},{4,5},{5,6},{6,7},{7,8},{8,9},{9,10},{10,1... | collective-permute-start | bytes 1544 | tf_op jit(solution)/shard_map/while/body/eval_jaxpr/ppermute | solution.py:18
  147.9 10.7 %collective-permute-start = (bf16[128,512]{1,0:T(8,128)(2,1)S(1)}, bf16[128,512]{1,0:T(8,128)(2,1)S(1)}, u32[]{:S(2)}, u32[]{:S(2)}) collective-permute-start(bf16[128,512]{1,0:T(8,128)(2,1)S(1)} %get-tuple-element.1222), channel_id=1, source_target_pairs={{0,1},{1,2},{2,3},{3,4},{4,5},{5,6},{6,7},{7,8},{8,9},{9,10},{10,1... | collective-permute-start | bytes 393224 | tf_op jit(solution)/shard_map/while/body/eval_jaxpr/ppermute | solution.py:18
  149.8 8.8 %collective-permute-start.1 = (s32[128]{0:T(128)S(1)}, s32[128]{0:T(128)S(1)}, u32[]{:S(2)}, u32[]{:S(2)}) collective-permute-start(s32[128]{0:T(128)S(1)} %get-tuple-element.1223), channel_id=1, source_target_pairs={{0,1},{1,2},{2,3},{3,4},{4,5},{5,6},{6,7},{7,8},{8,9},{9,10},{10,1... | collective-permute-start | bytes 1544 | tf_op jit(solution)/shard_map/while/body/eval_jaxpr/ppermute | solution.py:18
  159.3 10.7 %collective-permute-start = (bf16[128,512]{1,0:T(8,128)(2,1)S(1)}, bf16[128,512]{1,0:T(8,128)(2,1)S(1)}, u32[]{:S(2)}, u32[]{:S(2)}) collective-permute-start(bf16[128,512]{1,0:T(8,128)(2,1)S(1)} %get-tuple-element.1222), channel_id=1, source_target_pairs={{0,1},{1,2},{2,3},{3,4},{4,5},{5,6},{6,7},{7,8},{8,9},{9,10},{10,1... | collective-permute-start | bytes 393224 | tf_op jit(solution)/shard_map/while/body/eval_jaxpr/ppermute | solution.py:18
  161.2 8.8 %collective-permute-start.1 = (s32[128]{0:T(128)S(1)}, s32[128]{0:T(128)S(1)}, u32[]{:S(2)}, u32[]{:S(2)}) collective-permute-start(s32[128]{0:T(128)S(1)} %get-tuple-element.1223), channel_id=1, source_target_pairs={{0,1},{1,2},{2,3},{3,4},{4,5},{5,6},{6,7},{7,8},{8,9},{9,10},{10,1... | collective-permute-start | bytes 1544 | tf_op jit(solution)/shard_map/while/body/eval_jaxpr/ppermute | solution.py:18
  170.7 10.7 %collective-permute-start = (bf16[128,512]{1,0:T(8,128)(2,1)S(1)}, bf16[128,512]{1,0:T(8,128)(2,1)S(1)}, u32[]{:S(2)}, u32[]{:S(2)}) collective-permute-start(bf16[128,512]{1,0:T(8,128)(2,1)S(1)} %get-tuple-element.1222), channel_id=1, source_target_pairs={{0,1},{1,2},{2,3},{3,4},{4,5},{5,6},{6,7},{7,8},{8,9},{9,10},{10,1... | collective-permute-start | bytes 393224 | tf_op jit(solution)/shard_map/while/body/eval_jaxpr/ppermute | solution.py:18
  172.6 8.8 %collective-permute-start.1 = (s32[128]{0:T(128)S(1)}, s32[128]{0:T(128)S(1)}, u32[]{:S(2)}, u32[]{:S(2)}) collective-permute-start(s32[128]{0:T(128)S(1)} %get-tuple-element.1223), channel_id=1, source_target_pairs={{0,1},{1,2},{2,3},{3,4},{4,5},{5,6},{6,7},{7,8},{8,9},{9,10},{10,1... | collective-permute-start | bytes 1544 | tf_op jit(solution)/shard_map/while/body/eval_jaxpr/ppermute | solution.py:18
  209.4 0.9 copy-start
  257.8 10.0 %collective-permute-start.2 = (f32[128,512]{1,0:T(8,128)S(1)}, f32[128,512]{1,0:T(8,128)S(1)}, u32[]{:S(2)}, u32[]{:S(2)}) collective-permute-start(f32[128,512]{1,0:T(8,128)S(1)} %get-tuple-element.1333), channel_id=1, source_target_pairs={{1,0},{2,1},{3,2},{4,3},{5,4},{6,5},{7,6},{8,7},{9,8},{10,9},{11,1... | collective-permute-start | bytes 786440 | tf_op jit(solution)/shard_map/while/body/eval_jaxpr/ppermute | solution.py:18
  268.8 9.5 %collective-permute-start.2 = (f32[128,512]{1,0:T(8,128)S(1)}, f32[128,512]{1,0:T(8,128)S(1)}, u32[]{:S(2)}, u32[]{:S(2)}) collective-permute-start(f32[128,512]{1,0:T(8,128)S(1)} %get-tuple-element.1333), channel_id=1, source_target_pairs={{1,0},{2,1},{3,2},{4,3},{5,4},{6,5},{7,6},{8,7},{9,8},{10,9},{11,1... | collective-permute-start | bytes 786440 | tf_op jit(solution)/shard_map/while/body/eval_jaxpr/ppermute | solution.py:18
  279.3 11.9 %collective-permute-start.2 = (f32[128,512]{1,0:T(8,128)S(1)}, f32[128,512]{1,0:T(8,128)S(1)}, u32[]{:S(2)}, u32[]{:S(2)}) collective-permute-start(f32[128,512]{1,0:T(8,128)S(1)} %get-tuple-element.1333), channel_id=1, source_target_pairs={{1,0},{2,1},{3,2},{4,3},{5,4},{6,5},{7,6},{8,7},{9,8},{10,9},{11,1... | collective-permute-start | bytes 786440 | tf_op jit(solution)/shard_map/while/body/eval_jaxpr/ppermute | solution.py:18
  292.2 13.2 %collective-permute-start.2 = (f32[128,512]{1,0:T(8,128)S(1)}, f32[128,512]{1,0:T(8,128)S(1)}, u32[]{:S(2)}, u32[]{:S(2)}) collective-permute-start(f32[128,512]{1,0:T(8,128)S(1)} %get-tuple-element.1333), channel_id=1, source_target_pairs={{1,0},{2,1},{3,2},{4,3},{5,4},{6,5},{7,6},{8,7},{9,8},{10,9},{11,1... | collective-permute-start | bytes 786440 | tf_op jit(solution)/shard_map/while/body/eval_jaxpr/ppermute | solution.py:18
  306.5 14.4 %collective-permute-start.2 = (f32[128,512]{1,0:T(8,128)S(1)}, f32[128,512]{1,0:T(8,128)S(1)}, u32[]{:S(2)}, u32[]{:S(2)}) collective-permute-start(f32[128,512]{1,0:T(8,128)S(1)} %get-tuple-element.1333), channel_id=1, source_target_pairs={{1,0},{2,1},{3,2},{4,3},{5,4},{6,5},{7,6},{8,7},{9,8},{10,9},{11,1... | collective-permute-start | bytes 786440 | tf_op jit(solution)/shard_map/while/body/eval_jaxpr/ppermute | solution.py:18
  321.8 13.5 %collective-permute-start.2 = (f32[128,512]{1,0:T(8,128)S(1)}, f32[128,512]{1,0:T(8,128)S(1)}, u32[]{:S(2)}, u32[]{:S(2)}) collective-permute-start(f32[128,512]{1,0:T(8,128)S(1)} %get-tuple-element.1333), channel_id=1, source_target_pairs={{1,0},{2,1},{3,2},{4,3},{5,4},{6,5},{7,6},{8,7},{9,8},{10,9},{11,1... | collective-permute-start | bytes 786440 | tf_op jit(solution)/shard_map/while/body/eval_jaxpr/ppermute | solution.py:18
  336.3 12.7 %collective-permute-start.2 = (f32[128,512]{1,0:T(8,128)S(1)}, f32[128,512]{1,0:T(8,128)S(1)}, u32[]{:S(2)}, u32[]{:S(2)}) collective-permute-start(f32[128,512]{1,0:T(8,128)S(1)} %get-tuple-element.1333), channel_id=1, source_target_pairs={{1,0},{2,1},{3,2},{4,3},{5,4},{6,5},{7,6},{8,7},{9,8},{10,9},{11,1... | collective-permute-start | bytes 786440 | tf_op jit(solution)/shard_map/while/body/eval_jaxpr/ppermute | solution.py:18
  350.1 11.8 %collective-permute-start.2 = (f32[128,512]{1,0:T(8,128)S(1)}, f32[128,512]{1,0:T(8,128)S(1)}, u32[]{:S(2)}, u32[]{:S(2)}) collective-permute-start(f32[128,512]{1,0:T(8,128)S(1)} %get-tuple-element.1333), channel_id=1, source_target_pairs={{1,0},{2,1},{3,2},{4,3},{5,4},{6,5},{7,6},{8,7},{9,8},{10,9},{11,1... | collective-permute-start | bytes 786440 | tf_op jit(solution)/shard_map/while/body/eval_jaxpr/ppermute | solution.py:18
  362.8 11.6 %collective-permute-start.2 = (f32[128,512]{1,0:T(8,128)S(1)}, f32[128,512]{1,0:T(8,128)S(1)}, u32[]{:S(2)}, u32[]{:S(2)}) collective-permute-start(f32[128,512]{1,0:T(8,128)S(1)} %get-tuple-element.1333), channel_id=1, source_target_pairs={{1,0},{2,1},{3,2},{4,3},{5,4},{6,5},{7,6},{8,7},{9,8},{10,9},{11,1... | collective-permute-start | bytes 786440 | tf_op jit(solution)/shard_map/while/body/eval_jaxpr/ppermute | solution.py:18
  375.4 11.6 %collective-permute-start.2 = (f32[128,512]{1,0:T(8,128)S(1)}, f32[128,512]{1,0:T(8,128)S(1)}, u32[]{:S(2)}, u32[]{:S(2)}) collective-permute-start(f32[128,512]{1,0:T(8,128)S(1)} %get-tuple-element.1333), channel_id=1, source_target_pairs={{1,0},{2,1},{3,2},{4,3},{5,4},{6,5},{7,6},{8,7},{9,8},{10,9},{11,1... | collective-permute-start | bytes 786440 | tf_op jit(solution)/shard_map/while/body/eval_jaxpr/ppermute | solution.py:18
  388.0 11.6 %collective-permute-start.2 = (f32[128,512]{1,0:T(8,128)S(1)}, f32[128,512]{1,0:T(8,128)S(1)}, u32[]{:S(2)}, u32[]{:S(2)}) collective-permute-start(f32[128,512]{1,0:T(8,128)S(1)} %get-tuple-element.1333), channel_id=1, source_target_pairs={{1,0},{2,1},{3,2},{4,3},{5,4},{6,5},{7,6},{8,7},{9,8},{10,9},{11,1... | collective-permute-start | bytes 786440 | tf_op jit(solution)/shard_map/while/body/eval_jaxpr/ppermute | solution.py:18
  400.6 11.6 %collective-permute-start.2 = (f32[128,512]{1,0:T(8,128)S(1)}, f32[128,512]{1,0:T(8,128)S(1)}, u32[]{:S(2)}, u32[]{:S(2)}) collective-permute-start(f32[128,512]{1,0:T(8,128)S(1)} %get-tuple-element.1333), channel_id=1, source_target_pairs={{1,0},{2,1},{3,2},{4,3},{5,4},{6,5},{7,6},{8,7},{9,8},{10,9},{11,1... | collective-permute-start | bytes 786440 | tf_op jit(solution)/shard_map/while/body/eval_jaxpr/ppermute | solution.py:18
  413.2 11.6 %collective-permute-start.2 = (f32[128,512]{1,0:T(8,128)S(1)}, f32[128,512]{1,0:T(8,128)S(1)}, u32[]{:S(2)}, u32[]{:S(2)}) collective-permute-start(f32[128,512]{1,0:T(8,128)S(1)} %get-tuple-element.1333), channel_id=1, source_target_pairs={{1,0},{2,1},{3,2},{4,3},{5,4},{6,5},{7,6},{8,7},{9,8},{10,9},{11,1... | collective-permute-start | bytes 786440 | tf_op jit(solution)/shard_map/while/body/eval_jaxpr/ppermute | solution.py:18
  425.8 11.6 %collective-permute-start.2 = (f32[128,512]{1,0:T(8,128)S(1)}, f32[128,512]{1,0:T(8,128)S(1)}, u32[]{:S(2)}, u32[]{:S(2)}) collective-permute-start(f32[128,512]{1,0:T(8,128)S(1)} %get-tuple-element.1333), channel_id=1, source_target_pairs={{1,0},{2,1},{3,2},{4,3},{5,4},{6,5},{7,6},{8,7},{9,8},{10,9},{11,1... | collective-permute-start | bytes 786440 | tf_op jit(solution)/shard_map/while/body/eval_jaxpr/ppermute | solution.py:18
  438.4 11.6 %collective-permute-start.2 = (f32[128,512]{1,0:T(8,128)S(1)}, f32[128,512]{1,0:T(8,128)S(1)}, u32[]{:S(2)}, u32[]{:S(2)}) collective-permute-start(f32[128,512]{1,0:T(8,128)S(1)} %get-tuple-element.1333), channel_id=1, source_target_pairs={{1,0},{2,1},{3,2},{4,3},{5,4},{6,5},{7,6},{8,7},{9,8},{10,9},{11,1... | collective-permute-start | bytes 786440 | tf_op jit(solution)/shard_map/while/body/eval_jaxpr/ppermute | solution.py:18
